TPU v7x, 128 devices: a whole 4x4x4 slice. The times are simulated.
128 devices in a mesh: replica: 8 (over y, z_hi), shard: 16 (over z_lo, x, core).
Axes of the slice: x: 4, y: 4, z: 4 (z_hi: 2, z_lo: 2; z = z_hi * 2 + z_lo), core: 2. Of those that a mesh axis runs over, the one named last changes fastest.
Arguments:
- images: float32 [384, 7, 7, 1024], P(('replica', 'shard')), may hold values from -6 to 6
- filters: float32 [1, 1024, 9216], P(None, 'shard'), may hold values from -0.0625 to 0.0625
- out_grad: float32 [384, 7, 7, 1024], P(('replica', 'shard')), may hold values from -6 to 6
Outputs:
- conv_out: float32 [384, 7, 7, 1024], P(('replica', 'shard'))
- filter_grad: float32 [1, 1024, 9216], P(None, 'shard', 'replica')
All inputs are finite; a program needn't handle non-finite values.
Results may differ from a plain program's by a relative error of at most 0.0003.
Values sent between devices are 32-bit elements; how exact they have to be, the bound alone decides.
A program may use at most 256 MiB of HBM per device.

v0:
```python
import jax
import jax.numpy as jnp
from jax import lax
from jax.sharding import PartitionSpec as P


def tap_terms(piece, grad_own, weight):
    count, rows, cols, width = piece.shape
    owned = weight.shape[0]
    padded = jnp.pad(piece, ((0, 0), (1, 1), (1, 1), (0, 0)))
    flat_grad = grad_own.reshape(-1, owned)
    output = jnp.zeros((count * rows * cols, owned), jnp.float32)
    pieces = []
    for a in range(3):
        for c in range(3):
            tap = 3 * a + c
            shifted = padded[:, a : a + rows, c : c + cols, :].reshape(-1, width)
            wslice = weight[:, tap * width : (tap + 1) * width]
            output = output + lax.dot_general(
                shifted,
                wslice,
                (((1,), (1,)), ((), ())),
                precision=lax.Precision.HIGHEST,
                preferred_element_type=jnp.float32,
            )
            pieces.append(
                lax.dot_general(
                    flat_grad,
                    shifted,
                    (((0,), (0,)), ((), ())),
                    precision=lax.Precision.HIGHEST,
                    preferred_element_type=jnp.float32,
                )
            )
    grad = jnp.stack(pieces, axis=0).transpose(1, 0, 2).reshape(owned, 9 * width)
    return (output.reshape(count, rows, cols, owned), grad)


def add_block(piece, grad_own, filters):
    output, grad = tap_terms(piece, grad_own[:, :, :, 0, :], filters[0])
    outs = [output]
    grads = [grad]
    stacked = jnp.stack(outs, axis=3)
    return (stacked, jnp.stack(grads, axis=0))


def on_device(images, filters, out_grad):
    img_dev, rows, cols, chans = images.shape
    groups, owned, kdim = filters.shape
    width = kdim // 9
    shaped = out_grad.reshape(img_dev, rows, cols, groups, width)
    grad_mine = lax.all_to_all(shaped, "shard", split_axis=4, concat_axis=0, tiled=True)
    conv_buf, grad_sum = add_block(
        lax.all_gather(images, "shard", axis=0, tiled=True), grad_mine, filters
    )
    returned = lax.all_to_all(conv_buf, "shard", split_axis=0, concat_axis=4, tiled=True)
    conv_out = returned.reshape(img_dev, rows, cols, chans)
    total = lax.psum(grad_sum, "replica")
    span = kdim // lax.axis_size("replica")
    filter_grad = lax.dynamic_slice_in_dim(total, lax.axis_index("replica") * span, span, 2)
    return (conv_out, filter_grad)


def solution(mesh):
    return jax.shard_map(
        on_device,
        mesh=mesh,
        in_specs=(
            P(("replica", "shard"), None, None, None),
            P(None, "shard", None),
            P(("replica", "shard"), None, None, None),
        ),
        out_specs=(P(("replica", "shard"), None, None, None), P(None, "shard", "replica")),
        check_vma=False,
    )
```

profile of v0, /device:TPU:8, one launch (start us, length us, event | category | flops | bytes accessed | tf_op | source)
XLA Modules:
  0.0 586.0 jit_solution(415974414344355399)
XLA Ops:
  7.2 0.7 all-gather.2.cloned.1.call-update
  7.9 23.6 %copy.27 = f32[3,7,7,1,1024]{2,3,1,0,4:T(1,128)} copy(f32[3,7,7,1,1024]{4,2,1,0,3:T(8,128)} %bitcast.125) | data formatting | bytes 1204224 | tf_op jit(solution)/shard_map/reshape | solution.py:51
  32.1 35.0 %reduce.4 = f32[1024,3,7,7]{3,2,1,0:T(8,128)} reduce(f32[1024,3,7,1,7]{4,3,2,1,0:T(1,128)} %bitcast.112, f32[]{:T(128)} %broadcast.3), dimensions={3}, to_apply=%bitcast.67.reduce_sub_computation | reduce | bytes 1204228
  67.1 9.2 %reshape.53 = f32[16,1,9408]{2,1,0:T(1,128)S(1)} reshape(f32[1024,3,7,7]{3,2,1,0:T(8,128)} %reduce.4) | data formatting | bytes 1204224
  76.3 17.4 %all_to_all.30 = f32[16,1,9408]{2,1,0:T(1,128)S(1)} all-to-all(f32[16,1,9408]{2,1,0:T(1,128)S(1)} %reshape.53), channel_id=1, replica_groups=mesh['replica'=8,'shard'=16] {'shard'}, dimensions={0} | all-to-all | bytes 1204224 | tf_op jit(solution)/shard_map/all_to_all | solution.py:52
  93.7 2.1 reduce.5
  95.7 19.8 %reshape.54 = f32[1024,3,7,1,7]{4,3,2,1,0:T(1,128)} reshape(f32[16,9408]{1,0:T(8,128)S(1)} %reduce.5) | data formatting | bytes 1204224
  115.5 37.1 %bitcast_reduce_fusion = f32[3,7,7,1024]{2,1,0,3:T(8,128)} fusion(f32[1024,3,7,1,7]{4,3,2,1,0:T(1,128)} %reshape.54), kind=kLoop, calls=%fused_computation.45 | loop fusion | bytes 1204224 | tf_op jit(solution)/shard_map/all_to_all | solution.py:52
  152.7 7.6 %copy.32 = f32[3,7,7,1,16,64]{5,4,3,2,1,0:T(8,128)S(1)} copy(f32[3,7,7,1,16,64]{2,1,0,5,4,3:T(8,128)} %bitcast.111) | data formatting | bytes 1204224 | tf_op jit(solution)/shard_map/all_to_all | solution.py:52
  160.9 57.5 %pad_slice_fusion = (f32[48,7,7,1024]{3,2,1,0:T(8,128)}, f32[48,7,7,1024]{3,2,1,0:T(8,128)}, f32[48,7,7,1024]{3,2,1,0:T(8,128)}, f32[48,7,7,1024]{3,2,1,0:T(8,12...) fusion(f32[48,7,7,1024]{3,2,1,0:T(8,128)} %all-gather.2.cloned., ...), kind=kLoop, calls=%fused_computation | loop fusion | bytes 86704128 | tf_op jit(solution)/shard_map/slice | solution.py:17
  218.4 11.0 %reshape.47 = f32[2352,1024]{1,0:T(8,128)} reshape(f32[48,7,7,1024]{3,2,1,0:T(8,128)} %get-tuple-element.2) | data formatting | bytes 19267584 | tf_op jit(solution)/shard_map/reshape | solution.py:17
  229.4 10.9 %reshape.40 = f32[2352,1024]{1,0:T(8,128)} reshape(f32[48,7,7,1024]{3,2,1,0:T(8,128)} %get-tuple-element.3) | data formatting | bytes 19267584 | tf_op jit(solution)/shard_map/reshape | solution.py:17
  240.3 10.9 %reshape.41 = f32[2352,1024]{1,0:T(8,128)} reshape(f32[48,7,7,1024]{3,2,1,0:T(8,128)} %get-tuple-element.4) | data formatting | bytes 19267584 | tf_op jit(solution)/shard_map/reshape | solution.py:17
  251.2 10.9 %reshape.42 = f32[2352,1024]{1,0:T(8,128)} reshape(f32[48,7,7,1024]{3,2,1,0:T(8,128)} %get-tuple-element.5) | data formatting | bytes 19267584 | tf_op jit(solution)/shard_map/reshape | solution.py:17
  262.1 11.0 %reshape.44 = f32[2352,1024]{1,0:T(8,128)} reshape(f32[48,7,7,1024]{3,2,1,0:T(8,128)} %get-tuple-element.6) | data formatting | bytes 19267584 | tf_op jit(solution)/shard_map/reshape | solution.py:17
  273.1 11.0 %reshape.45 = f32[2352,1024]{1,0:T(8,128)} reshape(f32[48,7,7,1024]{3,2,1,0:T(8,128)} %get-tuple-element.7) | data formatting | bytes 19267584 | tf_op jit(solution)/shard_map/reshape | solution.py:17
  284.1 10.9 %reshape.46 = f32[2352,1024]{1,0:T(8,128)} reshape(f32[48,7,7,1024]{3,2,1,0:T(8,128)} %get-tuple-element.8) | data formatting | bytes 19267584 | tf_op jit(solution)/shard_map/reshape | solution.py:17
  295.0 11.0 %reshape.39 = f32[2352,1024]{1,0:T(8,128)} reshape(f32[48,7,7,1024]{3,2,1,0:T(8,128)} %get-tuple-element.9) | data formatting | bytes 19267584 | tf_op jit(solution)/shard_map/reshape | solution.py:17
  306.0 14.4 %fusion.17 = f32[2352,64]{0,1:T(8,128)S(1)} fusion(f32[2352,1024]{1,0:T(8,128)} %reshape.39, f32[64,9216]{1,0:T(8,128)} %bitcast.116), kind=kOutput, calls=%fused_computation.42 | convolution fusion | flops 1849688064 | bytes 10498048 | tf_op jit(solution)/shard_map/dot_general | solution.py:19
  320.4 7.1 %fusion.8 = f32[9,64,1024]{2,1,0:T(8,128)} fusion(f32[2352,1024]{1,0:T(8,128)S(1)} %copy-done, f32[2352,64]{1,0:T(8,128)S(1)} %reshape_squeeze.3), kind=kOutput, calls=%fused_computation.33 | convolution fusion | flops 1849688064 | bytes 10498048 | tf_op jit(solution)/shard_map/dot_general | solution.py:27
  327.6 7.1 %fusion.7 = f32[9,64,1024]{2,1,0:T(8,128)} fusion(f32[9,64,1024]{2,1,0:T(8,128)} %fusion.8, f32[2352,1024]{1,0:T(8,128)S(1)} %bitcast.110, f32[2352,64]{1,0:T(8,128)S(1)} %reshape_squeeze.3), kind=kOutput, calls=%fused_computation.31 | convolution fusion | flops 1849688064 | bytes 10498048 | tf_op jit(solution)/shard_map/dot_general | solution.py:27
  334.7 10.6 %convolution_add_fusion.7 = f32[2352,64]{0,1:T(8,128)S(1)} fusion(f32[2352,64]{0,1:T(8,128)S(1)} %fusion.17, f32[2352,1024]{1,0:T(8,128)S(1)} %bitcast.110, f32[64,9216]{1,0:T(8,128)} %bitcast.117), kind=kOutput, calls=%fused_computation.15 | convolution fusion | flops 1849838592 | bytes 11100160 | tf_op jit(solution)/shard_map/dot_general | solution.py:19
  345.4 10.7 %convolution_add_fusion.6 = f32[2352,64]{0,1:T(8,128)S(1)} fusion(f32[2352,64]{0,1:T(8,128)S(1)} %convolution_add_fusion.7, f32[2352,1024]{1,0:T(8,128)S(1)} %bitcast.108, f32[64,9216]{1,0:T(8,128)} %bitcast.118), kind=kOutput, calls=%fused_computation.14 | convolution fusion | flops 1849838592 | bytes 11100160 | tf_op jit(solution)/shard_map/dot_general | solution.py:19
  356.1 7.1 %fusion.6 = f32[9,64,1024]{2,1,0:T(8,128)} fusion(f32[9,64,1024]{2,1,0:T(8,128)} %fusion.7, f32[2352,1024]{1,0:T(8,128)S(1)} %bitcast.108, f32[2352,64]{1,0:T(8,128)S(1)} %reshape_squeeze.3), kind=kOutput, calls=%fused_computation.29 | convolution fusion | flops 1849688064 | bytes 10498048 | tf_op jit(solution)/shard_map/dot_general | solution.py:27
  363.3 7.5 %fusion.5 = f32[9,64,1024]{2,1,0:T(8,128)} fusion(f32[9,64,1024]{2,1,0:T(8,128)} %fusion.6, f32[2352,1024]{1,0:T(8,128)S(1)} %bitcast.106, f32[2352,64]{1,0:T(8,128)S(1)} %reshape_squeeze.3), kind=kOutput, calls=%fused_computation.27 | convolution fusion | flops 1849688064 | bytes 10498048 | tf_op jit(solution)/shard_map/dot_general | solution.py:27
  370.8 10.3 %convolution_add_fusion.5 = f32[2352,64]{0,1:T(8,128)S(1)} fusion(f32[2352,64]{0,1:T(8,128)S(1)} %convolution_add_fusion.6, f32[2352,1024]{1,0:T(8,128)S(1)} %bitcast.106, f32[64,9216]{1,0:T(8,128)} %bitcast.119), kind=kOutput, calls=%fused_computation.13 | convolution fusion | flops 1849838592 | bytes 11100160 | tf_op jit(solution)/shard_map/dot_general | solution.py:19
  381.2 11.0 %reshape.43 = f32[2352,1024]{1,0:T(8,128)} reshape(f32[48,7,7,1024]{3,2,1,0:T(8,128)} %all-gather.2.cloned.1.call-done) | data formatting | bytes 19267584 | tf_op jit(solution)/shard_map/reshape | solution.py:17
  392.1 14.2 %convolution_add_fusion.4 = f32[2352,64]{0,1:T(8,128)S(1)} fusion(f32[2352,64]{0,1:T(8,128)S(1)} %convolution_add_fusion.5, f32[2352,1024]{1,0:T(8,128)} %reshape.43, f32[64,9216]{1,0:T(8,128)} %bitcast.120), kind=kOutput, calls=%fused_computation.12 | convolution fusion | flops 1849838592 | bytes 11100160 | tf_op jit(solution)/shard_map/dot_general | solution.py:19
  406.4 6.8 %fusion.4 = f32[9,64,1024]{2,1,0:T(8,128)} fusion(f32[9,64,1024]{2,1,0:T(8,128)} %fusion.5, f32[2352,64]{1,0:T(8,128)S(1)} %reshape_squeeze.3, f32[2352,1024]{1,0:T(8,128)S(1)} %copy-done.1), kind=kOutput, calls=%fused_computation.25 | convolution fusion | flops 1849688064 | bytes 10498048 | tf_op jit(solution)/shard_map/dot_general | solution.py:27
  413.2 10.0 %fusion.3 = f32[9,64,1024]{2,1,0:T(8,128)} fusion(f32[9,64,1024]{2,1,0:T(8,128)} %fusion.4, f32[2352,1024]{1,0:T(8,128)} %reshape.44, f32[2352,64]{1,0:T(8,128)S(1)} %reshape_squeeze.3), kind=kOutput, calls=%fused_computation.23 | convolution fusion | flops 1849688064 | bytes 10498048 | tf_op jit(solution)/shard_map/dot_general | solution.py:27
  423.3 7.2 %fusion.2 = f32[9,64,1024]{2,1,0:T(8,128)} fusion(f32[9,64,1024]{2,1,0:T(8,128)} %fusion.3, f32[2352,1024]{1,0:T(8,128)S(1)} %bitcast.104, f32[2352,64]{1,0:T(8,128)S(1)} %reshape_squeeze.3), kind=kOutput, calls=%fused_computation.21 | convolution fusion | flops 1849688064 | bytes 10498048 | tf_op jit(solution)/shard_map/dot_general | solution.py:27
  430.5 7.1 %fusion.1 = f32[9,64,1024]{2,1,0:T(8,128)} fusion(f32[9,64,1024]{2,1,0:T(8,128)} %fusion.2, f32[2352,1024]{1,0:T(8,128)S(1)} %bitcast.102, f32[2352,64]{1,0:T(8,128)S(1)} %reshape_squeeze.3), kind=kOutput, calls=%fused_computation.19 | convolution fusion | flops 1849688064 | bytes 10498048 | tf_op jit(solution)/shard_map/dot_general | solution.py:27
  437.6 7.5 %fusion = f32[9,64,1024]{2,1,0:T(8,128)} fusion(f32[9,64,1024]{2,1,0:T(8,128)} %fusion.1, f32[2352,1024]{1,0:T(8,128)S(1)} %bitcast.98, f32[2352,64]{1,0:T(8,128)S(1)} %reshape_squeeze.3), kind=kOutput, calls=%fused_computation.17 | convolution fusion | flops 1849688064 | bytes 10498048 | tf_op jit(solution)/shard_map/dot_general | solution.py:27
  445.1 5.1 copy.30
  450.3 4.5 stack_reshape.7
  454.8 13.0 %convolution_add_fusion.3 = f32[2352,64]{0,1:T(8,128)S(1)} fusion(f32[2352,64]{0,1:T(8,128)S(1)} %convolution_add_fusion.4, f32[2352,1024]{1,0:T(8,128)} %reshape.44, f32[64,9216]{1,0:T(8,128)} %bitcast.121), kind=kOutput, calls=%fused_computation.11 | convolution fusion | flops 1849838592 | bytes 11100160 | tf_op jit(solution)/shard_map/dot_general | solution.py:19
  467.8 13.3 %convolution_add_fusion.2 = f32[2352,64]{0,1:T(8,128)S(1)} fusion(f32[2352,64]{0,1:T(8,128)S(1)} %convolution_add_fusion.3, f32[2352,1024]{1,0:T(8,128)} %reshape.45, f32[64,9216]{1,0:T(8,128)} %bitcast.122), kind=kOutput, calls=%fused_computation.10 | convolution fusion | flops 1849838592 | bytes 11100160 | tf_op jit(solution)/shard_map/dot_general | solution.py:19
  481.1 13.3 %convolution_add_fusion.1 = f32[2352,64]{0,1:T(8,128)S(1)} fusion(f32[2352,64]{0,1:T(8,128)S(1)} %convolution_add_fusion.2, f32[2352,1024]{1,0:T(8,128)} %reshape.46, f32[64,9216]{1,0:T(8,128)} %bitcast.123), kind=kOutput, calls=%fused_computation.9 | convolution fusion | flops 1849838592 | bytes 11100160 | tf_op jit(solution)/shard_map/dot_general | solution.py:19
  494.4 10.3 %convolution_add_fusion = f32[2352,64]{0,1:T(8,128)S(1)} fusion(f32[2352,64]{0,1:T(8,128)S(1)} %convolution_add_fusion.1, f32[2352,1024]{1,0:T(8,128)S(1)} %bitcast.100, f32[64,9216]{1,0:T(8,128)} %bitcast.124), kind=kOutput, calls=%fused_computation.8 | convolution fusion | flops 1849838592 | bytes 11100160 | tf_op jit(solution)/shard_map/dot_general | solution.py:19
  505.1 3.7 reduce.2
  508.8 1.8 reshape.51
  510.5 3.8 all-to-all-start
  514.4 11.7 %all-to-all-done = f32[16,1,9408]{2,1,0:T(1,128)S(1)} async-done(((f32[16,1,9408]{2,1,0:T(1,128)}), f32[16,1,9408]{2,1,0:T(1,128)S(1)}, u32[]{:S(2)}, u32[]{:S(2)}) %all-to-all-start) | async-done | bytes 602144 | tf_op jit(solution)/shard_map/all_to_all | solution.py:56
  526.1 2.1 reduce.3
  528.2 1.2 reshape.52
  529.5 1.2 reshape.48
  530.8 46.4 %all-reduce.3.cloned.1.call-done = f32[1,64,9216]{2,1,0:T(8,128)} async-done(((f32[1,64,9216]{2,1,0:T(8,128)}), f32[1,64,9216]{2,1,0:T(8,128)}) %all-reduce.3.cloned.1.call-update) | async-done | bytes 2359312 | tf_op jit(solution)/shard_map/psum | solution.py:58
  577.2 1.7 constant_dynamic-slice_fusion
  (62 shorter events, 1.8 us)
Async XLA Ops:
  7.2 153.7 %all-gather.2.cloned.1.call-start = ((), (), s32[]{:S(2)}) async-start(), calls=%async_computation.2 | async-start | bytes 11698176 | tf_op jit(solution)/shard_map/all_gather | solution.py:54
  7.9 569.3 %all-reduce.3.cloned.1.call-start = ((), (), s32[]{:S(2)}) async-start(), calls=%async_computation.3 | async-start | bytes 4718592 | tf_op jit(solution)/shard_map/psum | solution.py:58
  306.0 14.5 %copy-start = (f32[2352,1024]{1,0:T(8,128)S(1)}, f32[2352,1024]{1,0:T(8,128)}, u32[]{:S(2)}) copy-start(f32[2352,1024]{1,0:T(8,128)} %reshape.39) | copy-start | bytes 28901380
  306.0 21.6 %slice-start.18 = ((s8[9633792]{0:T(1024)(128)(4,1)}), s8[4194304]{0:T(1024)(128)(4,1)S(1)}, s32[]{:S(2)}) async-start(s8[9633792]{0:T(1024)(128)(4,1)} %bitcast.109), calls=%async_computation.22 | async-start | bytes 8388608
  306.0 21.6 %slice-start.19 = ((s8[9633792]{0:T(1024)(128)(4,1)}), s8[4194304]{0:T(1024)(128)(4,1)S(1)}, s32[]{:S(2)}) async-start(s8[9633792]{0:T(1024)(128)(4,1)} %bitcast.109), calls=%async_computation.23 | async-start | bytes 8388608
  320.4 7.1 %slice-start.20 = ((s8[9633792]{0:T(1024)(128)(4,1)}), s8[1245184]{0:T(1024)(128)(4,1)S(1)}, s32[]{:S(2)}) async-start(s8[9633792]{0:T(1024)(128)(4,1)} %bitcast.109), calls=%async_computation.24 | async-start | bytes 2490368
  327.6 17.8 %slice-start.15 = ((s8[9633792]{0:T(1024)(128)(4,1)}), s8[4194304]{0:T(1024)(128)(4,1)S(1)}, s32[]{:S(2)}) async-start(s8[9633792]{0:T(1024)(128)(4,1)} %bitcast.107), calls=%async_computation.19 | async-start | bytes 8388608
  327.6 17.8 %slice-start.16 = ((s8[9633792]{0:T(1024)(128)(4,1)}), s8[4194304]{0:T(1024)(128)(4,1)S(1)}, s32[]{:S(2)}) async-start(s8[9633792]{0:T(1024)(128)(4,1)} %bitcast.107), calls=%async_computation.20 | async-start | bytes 8388608
  334.7 10.6 %slice-start.17 = ((s8[9633792]{0:T(1024)(128)(4,1)}), s8[1245184]{0:T(1024)(128)(4,1)S(1)}, s32[]{:S(2)}) async-start(s8[9633792]{0:T(1024)(128)(4,1)} %bitcast.107), calls=%async_computation.21 | async-start | bytes 2490368
  345.4 17.9 %slice-start.12 = ((s8[9633792]{0:T(1024)(128)(4,1)}), s8[4194304]{0:T(1024)(128)(4,1)S(1)}, s32[]{:S(2)}) async-start(s8[9633792]{0:T(1024)(128)(4,1)} %bitcast.105), calls=%async_computation.16 | async-start | bytes 8388608
  345.4 17.9 %slice-start.13 = ((s8[9633792]{0:T(1024)(128)(4,1)}), s8[4194304]{0:T(1024)(128)(4,1)S(1)}, s32[]{:S(2)}) async-start(s8[9633792]{0:T(1024)(128)(4,1)} %bitcast.105), calls=%async_computation.17 | async-start | bytes 8388608
  356.1 7.2 %slice-start.14 = ((s8[9633792]{0:T(1024)(128)(4,1)}), s8[1245184]{0:T(1024)(128)(4,1)S(1)}, s32[]{:S(2)}) async-start(s8[9633792]{0:T(1024)(128)(4,1)} %bitcast.105), calls=%async_computation.18 | async-start | bytes 2490368
  392.1 14.2 %copy-start.1 = (f32[2352,1024]{1,0:T(8,128)S(1)}, f32[2352,1024]{1,0:T(8,128)}, u32[]{:S(2)}) copy-start(f32[2352,1024]{1,0:T(8,128)} %reshape.43) | copy-start | bytes 28901380
  406.3 16.9 %slice-start.9 = ((s8[9633792]{0:T(1024)(128)(4,1)}), s8[4194304]{0:T(1024)(128)(4,1)S(1)}, s32[]{:S(2)}) async-start(s8[9633792]{0:T(1024)(128)(4,1)} %bitcast.103), calls=%async_computation.13 | async-start | bytes 8388608
  406.4 16.9 %slice-start.10 = ((s8[9633792]{0:T(1024)(128)(4,1)}), s8[4194304]{0:T(1024)(128)(4,1)S(1)}, s32[]{:S(2)}) async-start(s8[9633792]{0:T(1024)(128)(4,1)} %bitcast.103), calls=%async_computation.14 | async-start | bytes 8388608
  413.2 10.0 %slice-start.11 = ((s8[9633792]{0:T(1024)(128)(4,1)}), s8[1245184]{0:T(1024)(128)(4,1)S(1)}, s32[]{:S(2)}) async-start(s8[9633792]{0:T(1024)(128)(4,1)} %bitcast.103), calls=%async_computation.15 | async-start | bytes 2490368
  413.2 17.2 %slice-start.6 = ((s8[9633792]{0:T(1024)(128)(4,1)}), s8[4194304]{0:T(1024)(128)(4,1)S(1)}, s32[]{:S(2)}) async-start(s8[9633792]{0:T(1024)(128)(4,1)} %bitcast.101), calls=%async_computation.10 | async-start | bytes 8388608
  413.2 17.2 %slice-start.7 = ((s8[9633792]{0:T(1024)(128)(4,1)}), s8[4194304]{0:T(1024)(128)(4,1)S(1)}, s32[]{:S(2)}) async-start(s8[9633792]{0:T(1024)(128)(4,1)} %bitcast.101), calls=%async_computation.11 | async-start | bytes 8388608
  423.2 7.2 %slice-start.8 = ((s8[9633792]{0:T(1024)(128)(4,1)}), s8[1245184]{0:T(1024)(128)(4,1)S(1)}, s32[]{:S(2)}) async-start(s8[9633792]{0:T(1024)(128)(4,1)} %bitcast.101), calls=%async_computation.12 | async-start | bytes 2490368
  423.3 14.3 %slice-start = ((s8[9633792]{0:T(1024)(128)(4,1)}), s8[4194304]{0:T(1024)(128)(4,1)S(1)}, s32[]{:S(2)}) async-start(s8[9633792]{0:T(1024)(128)(4,1)} %bitcast.97), calls=%async_computation.4 | async-start | bytes 8388608
  423.3 14.3 %slice-start.1 = ((s8[9633792]{0:T(1024)(128)(4,1)}), s8[4194304]{0:T(1024)(128)(4,1)S(1)}, s32[]{:S(2)}) async-start(s8[9633792]{0:T(1024)(128)(4,1)} %bitcast.97), calls=%async_computation.5 | async-start | bytes 8388608
  430.4 7.2 %slice-start.2 = ((s8[9633792]{0:T(1024)(128)(4,1)}), s8[1245184]{0:T(1024)(128)(4,1)S(1)}, s32[]{:S(2)}) async-start(s8[9633792]{0:T(1024)(128)(4,1)} %bitcast.97), calls=%async_computation.6 | async-start | bytes 2490368
  467.7 26.6 %slice-start.3 = ((s8[9633792]{0:T(1024)(128)(4,1)}), s8[4194304]{0:T(1024)(128)(4,1)S(1)}, s32[]{:S(2)}) async-start(s8[9633792]{0:T(1024)(128)(4,1)} %bitcast.99), calls=%async_computation.7 | async-start | bytes 8388608
  467.7 26.6 %slice-start.4 = ((s8[9633792]{0:T(1024)(128)(4,1)}), s8[4194304]{0:T(1024)(128)(4,1)S(1)}, s32[]{:S(2)}) async-start(s8[9633792]{0:T(1024)(128)(4,1)} %bitcast.99), calls=%async_computation.8 | async-start | bytes 8388608
  481.1 13.3 %slice-start.5 = ((s8[9633792]{0:T(1024)(128)(4,1)}), s8[1245184]{0:T(1024)(128)(4,1)S(1)}, s32[]{:S(2)}) async-start(s8[9633792]{0:T(1024)(128)(4,1)} %bitcast.99), calls=%async_computation.9 | async-start | bytes 2490368
  510.5 15.5 %all-to-all-start = ((f32[16,1,9408]{2,1,0:T(1,128)}), f32[16,1,9408]{2,1,0:T(1,128)S(1)}, u32[]{:S(2)}, u32[]{:S(2)}) async-start(f32[16,1,9408]{2,1,0:T(1,128)} %reshape.51), calls=%async_computation | async-start | bytes 1212416 | tf_op jit(solution)/shard_map/all_to_all | solution.py:56
Sparse Core Ops, SparseCore 0:
  9.7 66.7 all-gather.1
  454.9 122.2 all-reduce.2
where the time goes:
time: 595 us; the launch traced here: 586 us
  local copies, waits for them, and re-layouts  271 us (46%)
  matrix products  178 us (30%)
  waiting for transfers between devices  58.8 us (10%)
  other arithmetic  42.9 us (7%)
  blocking collectives  17.4 us (3%)
  between operations  14.7 us (2%)
    dot_general x9, matrix products, tap_terms(): lax.dot_general(shifted, wslice, (((1,), (1,)), ((), ())), precision=lax....  110 us
    reshape x9, local copies, waits for them, and re-layouts, tap_terms(): shifted = padded[:, a:a + rows, c:c + cols, :].reshape(-1, width)  98.5 us
    dot_general x9, matrix products, tap_terms(): lax.dot_general(flat_grad, shifted, (((0,), (0,)), ((), ())), precision=l...  67.6 us
    slice x1, local copies, waits for them, and re-layouts, tap_terms(): shifted = padded[:, a:a + rows, c:c + cols, :].reshape(-1, width)  57.5 us
    psum x1, waiting for transfers between devices, on_device(): total = lax.psum(grad_sum, 'replica')  46.4 us
    all_to_all x3, local copies, waits for them, and re-layouts, on_device(): lax.all_to_all(shaped, 'shard', split_axis=4, concat_axis=0, tiled=True)  45.2 us
    unnamed x8, other arithmetic  35 us
    unnamed x50, local copies, waits for them, and re-layouts  32.1 us
  transfers between devices with their start and end apart: 3, of which 2 were waited for; matrix products, arithmetic and copies ran while one was open for 33% of the time, Pallas kernels for 0%

commit v1 on v0

--- a/solution.py
+++ b/solution.py
@@ -55,7 +55,7 @@
     )
     returned = lax.all_to_all(conv_buf, "shard", split_axis=0, concat_axis=4, tiled=True)
     conv_out = returned.reshape(img_dev, rows, cols, chans)
-    total = lax.psum(grad_sum, "replica")
+    total = jnp.sum(lax.all_gather(grad_sum, "replica"), axis=0)
     span = kdim // lax.axis_size("replica")
     filter_grad = lax.dynamic_slice_in_dim(total, lax.axis_index("replica") * span, span, 2)
     return (conv_out, filter_grad)

time: 595 us -> 638 us (1.072)
  waiting for transfers between devices: 58.8 us -> 89.4 us
  other arithmetic: 42.9 us -> 50.6 us
    all_gather x0 -> x1, waiting for transfers between devices: none -> 77 us  [on_device(): total = jnp.sum(lax.all_gather(grad_sum, 'replica'), axis=0)]
    psum x1 -> x0, waiting for transfers between devices: 46.4 us -> none  [on_device(): total = lax.psum(grad_sum, 'replica')]
    dot_general x9, matrix products: 67.6 us -> 75.3 us  [tap_terms(): lax.dot_general(flat_grad, shifted, (((0,), (0,)), ((), ())), precision=l...]
    reduce_sum x0 -> x1, other arithmetic: none -> 7.73 us  [on_device(): total = jnp.sum(lax.all_gather(grad_sum, 'replica'), axis=0)]
    unnamed x8 -> x11, other arithmetic: 35 us -> 35 us
    unnamed x50 -> x64, local copies, waits for them, and re-layouts: 32.1 us -> 32.1 us
  transfers between devices with their start and end apart: 3 -> 3, of which waited for: 2 -> 2; matrix products, arithmetic and copies ran while one was open for 33% -> 40% of each run, Pallas kernels for 0% -> 0%
where the time goes in v1:
time: 638 us; the launch traced here: 628 us
  local copies, waits for them, and re-layouts  270 us (42%)
  matrix products  182 us (29%)
  waiting for transfers between devices  89.4 us (14%)
  other arithmetic  50.6 us (8%)
  blocking collectives  17.5 us (3%)
  between operations  14.8 us (2%)
    dot_general x9, matrix products, tap_terms(): lax.dot_general(shifted, wslice, (((1,), (1,)), ((), ())), precision=lax....  107 us
    reshape x9, local copies, waits for them, and re-layouts, tap_terms(): shifted = padded[:, a:a + rows, c:c + cols, :].reshape(-1, width)  98.4 us
    all_gather x1, waiting for transfers between devices, on_device(): total = jnp.sum(lax.all_gather(grad_sum, 'replica'), axis=0)  77 us
    dot_general x9, matrix products, tap_terms(): lax.dot_general(flat_grad, shifted, (((0,), (0,)), ((), ())), precision=l...  75.3 us
    slice x1, local copies, waits for them, and re-layouts, tap_terms(): shifted = padded[:, a:a + rows, c:c + cols, :].reshape(-1, width)  57.5 us
    all_to_all x3, local copies, waits for them, and re-layouts, on_device(): lax.all_to_all(shaped, 'shard', split_axis=4, concat_axis=0, tiled=True)  45.2 us
    unnamed x11, other arithmetic  35 us
    unnamed x64, local copies, waits for them, and re-layouts  32.1 us
  transfers between devices with their start and end apart: 3, of which 2 were waited for; matrix products, arithmetic and copies ran while one was open for 40% of the time, Pallas kernels for 0%

profile of v1, /device:TPU:8, one launch (start us, length us, event | category | flops | bytes accessed | tf_op | source)
XLA Modules:
  0.0 628.0 jit_solution(16987163443426252758)
XLA Ops:
  7.9 23.5 %copy.27 = f32[3,7,7,1,1024]{2,3,1,0,4:T(1,128)} copy(f32[3,7,7,1,1024]{4,2,1,0,3:T(8,128)} %bitcast.133) | data formatting | bytes 1204224 | tf_op jit(solution)/shard_map/reshape | solution.py:51
  32.0 35.0 %reduce.5 = f32[1024,3,7,7]{3,2,1,0:T(8,128)} reduce(f32[1024,3,7,1,7]{4,3,2,1,0:T(1,128)} %bitcast.120, f32[]{:T(128)} %broadcast.3), dimensions={3}, to_apply=%bitcast.69.reduce_sub_computation | reduce | bytes 1204228
  67.0 9.2 %reshape.55 = f32[16,1,9408]{2,1,0:T(1,128)S(1)} reshape(f32[1024,3,7,7]{3,2,1,0:T(8,128)} %reduce.5) | data formatting | bytes 1204224
  76.2 17.5 %all_to_all.30 = f32[16,1,9408]{2,1,0:T(1,128)S(1)} all-to-all(f32[16,1,9408]{2,1,0:T(1,128)S(1)} %reshape.55), channel_id=1, replica_groups=mesh['replica'=8,'shard'=16] {'shard'}, dimensions={0} | all-to-all | bytes 1204224 | tf_op jit(solution)/shard_map/all_to_all | solution.py:52
  93.7 2.1 reduce.6
  95.8 19.8 %reshape.56 = f32[1024,3,7,1,7]{4,3,2,1,0:T(1,128)} reshape(f32[16,9408]{1,0:T(8,128)S(1)} %reduce.6) | data formatting | bytes 1204224
  115.6 37.2 %bitcast_reduce_fusion = f32[3,7,7,1024]{2,1,0,3:T(8,128)} fusion(f32[1024,3,7,1,7]{4,3,2,1,0:T(1,128)} %reshape.56), kind=kLoop, calls=%fused_computation.45 | loop fusion | bytes 1204224 | tf_op jit(solution)/shard_map/all_to_all | solution.py:52
  152.8 7.6 %copy.32 = f32[3,7,7,1,16,64]{5,4,3,2,1,0:T(8,128)S(1)} copy(f32[3,7,7,1,16,64]{2,1,0,5,4,3:T(8,128)} %bitcast.119) | data formatting | bytes 1204224 | tf_op jit(solution)/shard_map/all_to_all | solution.py:52
  161.0 57.5 %pad_slice_fusion = (f32[48,7,7,1024]{3,2,1,0:T(8,128)}, f32[48,7,7,1024]{3,2,1,0:T(8,128)}, f32[48,7,7,1024]{3,2,1,0:T(8,128)}, f32[48,7,7,1024]{3,2,1,0:T(8,12...) fusion(f32[48,7,7,1024]{3,2,1,0:T(8,128)} %all-gather.3.cloned., ...), kind=kLoop, calls=%fused_computation | loop fusion | bytes 86704128 | tf_op jit(solution)/shard_map/slice | solution.py:17
  218.6 11.0 %reshape.49 = f32[2352,1024]{1,0:T(8,128)} reshape(f32[48,7,7,1024]{3,2,1,0:T(8,128)} %get-tuple-element.2) | data formatting | bytes 19267584 | tf_op jit(solution)/shard_map/reshape | solution.py:17
  229.5 10.9 %reshape.42 = f32[2352,1024]{1,0:T(8,128)} reshape(f32[48,7,7,1024]{3,2,1,0:T(8,128)} %get-tuple-element.3) | data formatting | bytes 19267584 | tf_op jit(solution)/shard_map/reshape | solution.py:17
  240.5 10.9 %reshape.43 = f32[2352,1024]{1,0:T(8,128)} reshape(f32[48,7,7,1024]{3,2,1,0:T(8,128)} %get-tuple-element.4) | data formatting | bytes 19267584 | tf_op jit(solution)/shard_map/reshape | solution.py:17
  251.4 11.0 %reshape.44 = f32[2352,1024]{1,0:T(8,128)} reshape(f32[48,7,7,1024]{3,2,1,0:T(8,128)} %get-tuple-element.5) | data formatting | bytes 19267584 | tf_op jit(solution)/shard_map/reshape | solution.py:17
  262.4 10.9 %reshape.46 = f32[2352,1024]{1,0:T(8,128)} reshape(f32[48,7,7,1024]{3,2,1,0:T(8,128)} %get-tuple-element.6) | data formatting | bytes 19267584 | tf_op jit(solution)/shard_map/reshape | solution.py:17
  273.3 10.9 %reshape.47 = f32[2352,1024]{1,0:T(8,128)} reshape(f32[48,7,7,1024]{3,2,1,0:T(8,128)} %get-tuple-element.7) | data formatting | bytes 19267584 | tf_op jit(solution)/shard_map/reshape | solution.py:17
  284.2 10.9 %reshape.48 = f32[2352,1024]{1,0:T(8,128)} reshape(f32[48,7,7,1024]{3,2,1,0:T(8,128)} %get-tuple-element.8) | data formatting | bytes 19267584 | tf_op jit(solution)/shard_map/reshape | solution.py:17
  295.1 10.9 %reshape.41 = f32[2352,1024]{1,0:T(8,128)} reshape(f32[48,7,7,1024]{3,2,1,0:T(8,128)} %get-tuple-element.9) | data formatting | bytes 19267584 | tf_op jit(solution)/shard_map/reshape | solution.py:17
  306.1 9.8 %fusion.8 = f32[9,64,1024]{2,1,0:T(8,128)} fusion(f32[2352,1024]{1,0:T(8,128)} %reshape.41, f32[2352,64]{1,0:T(8,128)S(1)} %reshape_squeeze.3), kind=kOutput, calls=%fused_computation.33 | convolution fusion | flops 1849688064 | bytes 10498048 | tf_op jit(solution)/shard_map/dot_general | solution.py:27
  315.9 9.9 %fusion.7 = f32[9,64,1024]{2,1,0:T(8,128)} fusion(f32[9,64,1024]{2,1,0:T(8,128)} %fusion.8, f32[2352,1024]{1,0:T(8,128)} %reshape.42, f32[2352,64]{1,0:T(8,128)S(1)} %reshape_squeeze.3), kind=kOutput, calls=%fused_computation.31 | convolution fusion | flops 1849688064 | bytes 10498048 | tf_op jit(solution)/shard_map/dot_general | solution.py:27
  325.9 7.2 %fusion.6 = f32[9,64,1024]{2,1,0:T(8,128)} fusion(f32[9,64,1024]{2,1,0:T(8,128)} %fusion.7, f32[2352,1024]{1,0:T(8,128)S(1)} %bitcast.118, f32[2352,64]{1,0:T(8,128)S(1)} %reshape_squeeze.3), kind=kOutput, calls=%fused_computation.29 | convolution fusion | flops 1849688064 | bytes 10498048 | tf_op jit(solution)/shard_map/dot_general | solution.py:27
  333.1 7.1 %fusion.5 = f32[9,64,1024]{2,1,0:T(8,128)} fusion(f32[9,64,1024]{2,1,0:T(8,128)} %fusion.6, f32[2352,1024]{1,0:T(8,128)S(1)} %bitcast.114, f32[2352,64]{1,0:T(8,128)S(1)} %reshape_squeeze.3), kind=kOutput, calls=%fused_computation.27 | convolution fusion | flops 1849688064 | bytes 10498048 | tf_op jit(solution)/shard_map/dot_general | solution.py:27
  340.2 10.9 %reshape.45 = f32[2352,1024]{1,0:T(8,128)} reshape(f32[48,7,7,1024]{3,2,1,0:T(8,128)} %all-gather.3.cloned.1.call-done) | data formatting | bytes 19267584 | tf_op jit(solution)/shard_map/reshape | solution.py:17
  351.2 9.5 %fusion.4 = f32[9,64,1024]{2,1,0:T(8,128)} fusion(f32[9,64,1024]{2,1,0:T(8,128)} %fusion.5, f32[2352,64]{1,0:T(8,128)S(1)} %reshape_squeeze.3, f32[2352,1024]{1,0:T(8,128)} %reshape.45), kind=kOutput, calls=%fused_computation.25 | convolution fusion | flops 1849688064 | bytes 10498048 | tf_op jit(solution)/shard_map/dot_general | solution.py:27
  360.6 10.2 %fusion.3 = f32[9,64,1024]{2,1,0:T(8,128)} fusion(f32[9,64,1024]{2,1,0:T(8,128)} %fusion.4, f32[2352,1024]{1,0:T(8,128)} %reshape.46, f32[2352,64]{1,0:T(8,128)S(1)} %reshape_squeeze.3), kind=kOutput, calls=%fused_computation.23 | convolution fusion | flops 1849688064 | bytes 10498048 | tf_op jit(solution)/shard_map/dot_general | solution.py:27
  370.9 7.1 %fusion.2 = f32[9,64,1024]{2,1,0:T(8,128)} fusion(f32[9,64,1024]{2,1,0:T(8,128)} %fusion.3, f32[2352,1024]{1,0:T(8,128)S(1)} %bitcast.108, f32[2352,64]{1,0:T(8,128)S(1)} %reshape_squeeze.3), kind=kOutput, calls=%fused_computation.21 | convolution fusion | flops 1849688064 | bytes 10498048 | tf_op jit(solution)/shard_map/dot_general | solution.py:27
  378.1 7.1 %fusion.1 = f32[9,64,1024]{2,1,0:T(8,128)} fusion(f32[9,64,1024]{2,1,0:T(8,128)} %fusion.2, f32[2352,1024]{1,0:T(8,128)S(1)} %bitcast.104, f32[2352,64]{1,0:T(8,128)S(1)} %reshape_squeeze.3), kind=kOutput, calls=%fused_computation.19 | convolution fusion | flops 1849688064 | bytes 10498048 | tf_op jit(solution)/shard_map/dot_general | solution.py:27
  385.2 7.3 %fusion = f32[9,64,1024]{2,1,0:T(8,128)} fusion(f32[9,64,1024]{2,1,0:T(8,128)} %fusion.1, f32[2352,1024]{1,0:T(8,128)S(1)} %bitcast.100, f32[2352,64]{1,0:T(8,128)S(1)} %reshape_squeeze.3), kind=kOutput, calls=%fused_computation.17 | convolution fusion | flops 1849688064 | bytes 10498048 | tf_op jit(solution)/shard_map/dot_general | solution.py:27
  392.5 5.1 copy.30
  397.7 4.6 all_gather_stack_reshape.3
  402.3 13.1 %fusion.17 = f32[2352,64]{0,1:T(8,128)S(1)} fusion(f32[2352,1024]{1,0:T(8,128)} %reshape.41, f32[64,9216]{1,0:T(8,128)} %bitcast.124), kind=kOutput, calls=%fused_computation.43 | convolution fusion | flops 1849688064 | bytes 10498048 | tf_op jit(solution)/shard_map/dot_general | solution.py:19
  415.4 14.0 %convolution_add_fusion.7 = f32[2352,64]{0,1:T(8,128)S(1)} fusion(f32[2352,64]{0,1:T(8,128)S(1)} %fusion.17, f32[2352,1024]{1,0:T(8,128)} %reshape.42, f32[64,9216]{1,0:T(8,128)} %bitcast.125), kind=kOutput, calls=%fused_computation.15 | convolution fusion | flops 1849838592 | bytes 11100160 | tf_op jit(solution)/shard_map/dot_general | solution.py:19
  429.5 13.5 %convolution_add_fusion.6 = f32[2352,64]{0,1:T(8,128)S(1)} fusion(f32[2352,64]{0,1:T(8,128)S(1)} %convolution_add_fusion.7, f32[2352,1024]{1,0:T(8,128)} %reshape.43, f32[64,9216]{1,0:T(8,128)} %bitcast.126), kind=kOutput, calls=%fused_computation.14 | convolution fusion | flops 1849838592 | bytes 11100160 | tf_op jit(solution)/shard_map/dot_general | solution.py:19
  443.1 10.5 %convolution_add_fusion.5 = f32[2352,64]{0,1:T(8,128)S(1)} fusion(f32[2352,64]{0,1:T(8,128)S(1)} %convolution_add_fusion.6, f32[2352,1024]{1,0:T(8,128)S(1)} %bitcast.116, f32[64,9216]{1,0:T(8,128)} %bitcast.127), kind=kOutput, calls=%fused_computation.13 | convolution fusion | flops 1849838592 | bytes 11100160 | tf_op jit(solution)/shard_map/dot_general | solution.py:19
  453.6 13.3 %convolution_add_fusion.4 = f32[2352,64]{0,1:T(8,128)S(1)} fusion(f32[2352,64]{0,1:T(8,128)S(1)} %convolution_add_fusion.5, f32[2352,1024]{1,0:T(8,128)} %reshape.45, f32[64,9216]{1,0:T(8,128)} %bitcast.128), kind=kOutput, calls=%fused_computation.12 | convolution fusion | flops 1849838592 | bytes 11100160 | tf_op jit(solution)/shard_map/dot_general | solution.py:19
  467.0 10.6 %convolution_add_fusion.3 = f32[2352,64]{0,1:T(8,128)S(1)} fusion(f32[2352,64]{0,1:T(8,128)S(1)} %convolution_add_fusion.4, f32[2352,1024]{1,0:T(8,128)S(1)} %bitcast.112, f32[64,9216]{1,0:T(8,128)} %bitcast.129), kind=kOutput, calls=%fused_computation.11 | convolution fusion | flops 1849838592 | bytes 11100160 | tf_op jit(solution)/shard_map/dot_general | solution.py:19
  477.6 10.7 %convolution_add_fusion.2 = f32[2352,64]{0,1:T(8,128)S(1)} fusion(f32[2352,64]{0,1:T(8,128)S(1)} %convolution_add_fusion.3, f32[2352,1024]{1,0:T(8,128)S(1)} %bitcast.110, f32[64,9216]{1,0:T(8,128)} %bitcast.130), kind=kOutput, calls=%fused_computation.10 | convolution fusion | flops 1849838592 | bytes 11100160 | tf_op jit(solution)/shard_map/dot_general | solution.py:19
  488.4 10.4 %convolution_add_fusion.1 = f32[2352,64]{0,1:T(8,128)S(1)} fusion(f32[2352,64]{0,1:T(8,128)S(1)} %convolution_add_fusion.2, f32[2352,1024]{1,0:T(8,128)S(1)} %bitcast.106, f32[64,9216]{1,0:T(8,128)} %bitcast.131), kind=kOutput, calls=%fused_computation.9 | convolution fusion | flops 1849838592 | bytes 11100160 | tf_op jit(solution)/shard_map/dot_general | solution.py:19
  498.9 10.7 %convolution_add_fusion = f32[2352,64]{0,1:T(8,128)S(1)} fusion(f32[2352,64]{0,1:T(8,128)S(1)} %convolution_add_fusion.1, f32[2352,1024]{1,0:T(8,128)S(1)} %bitcast.102, f32[64,9216]{1,0:T(8,128)} %bitcast.132), kind=kOutput, calls=%fused_computation.8 | convolution fusion | flops 1849838592 | bytes 11100160 | tf_op jit(solution)/shard_map/dot_general | solution.py:19
  510.0 3.7 reduce.3
  513.7 1.8 reshape.53
  515.4 3.8 all-to-all-start
  519.2 11.7 %all-to-all-done = f32[16,1,9408]{2,1,0:T(1,128)S(1)} async-done(((f32[16,1,9408]{2,1,0:T(1,128)}), f32[16,1,9408]{2,1,0:T(1,128)S(1)}, u32[]{:S(2)}, u32[]{:S(2)}) %all-to-all-start) | async-done | bytes 602144 | tf_op jit(solution)/shard_map/all_to_all | solution.py:56
  530.9 2.1 reduce.4
  533.0 1.2 reshape.54
  534.3 1.2 reshape.50
  535.5 77.0 %all-gather.5.cloned.1.call-done = f32[8,1,64,9216]{3,2,1,0:T(8,128)} async-done(((f32[1,1,64,9216]{3,2,1,0:T(8,128)}), f32[8,1,64,9216]{3,2,1,0:T(8,128)}) %all-gather.5.cloned.1.call-update) | async-done | bytes 18874384 | tf_op jit(solution)/shard_map/all_gather | solution.py:58
  612.5 7.7 %reduce_sum.9 = f32[64,9216]{1,0:T(8,128)S(1)} reduce(f32[8,1,64,9216]{3,2,1,0:T(8,128)} %all-gather.5.cloned.1.call-done, f32[]{:T(128)} %constant.3.clone.1), dimensions={0,1}, to_apply=%region_0.1 | reduce | flops 4128768 | bytes 21233668 | tf_op jit(solution)/shard_map/reduce_sum | solution.py:58
  620.3 0.7 dynamic-slice_bitcast_fusion
  (80 shorter events, 2.5 us)
Async XLA Ops:
  7.2 153.9 %all-gather.3.cloned.1.call-start = ((), (), s32[]{:S(2)}) async-start(), calls=%async_computation.2 | async-start | bytes 11698176 | tf_op jit(solution)/shard_map/all_gather | solution.py:54
  7.9 604.6 %all-gather.5.cloned.1.call-start = ((), (), s32[]{:S(2)}) async-start(), calls=%async_computation.3 | async-start | bytes 21233664 | tf_op jit(solution)/shard_map/all_gather | solution.py:58
  306.1 19.8 %slice-start.27 = ((s8[9633792]{0:T(1024)(128)(4,1)}), s8[4194304]{0:T(1024)(128)(4,1)S(1)}, s32[]{:S(2)}) async-start(s8[9633792]{0:T(1024)(128)(4,1)} %bitcast.117), calls=%async_computation.31 | async-start | bytes 8388608
  306.1 19.8 %slice-start.28 = ((s8[9633792]{0:T(1024)(128)(4,1)}), s8[4194304]{0:T(1024)(128)(4,1)S(1)}, s32[]{:S(2)}) async-start(s8[9633792]{0:T(1024)(128)(4,1)} %bitcast.117), calls=%async_computation.32 | async-start | bytes 8388608
  315.9 10.0 %slice-start.29 = ((s8[9633792]{0:T(1024)(128)(4,1)}), s8[1245184]{0:T(1024)(128)(4,1)S(1)}, s32[]{:S(2)}) async-start(s8[9633792]{0:T(1024)(128)(4,1)} %bitcast.117), calls=%async_computation.33 | async-start | bytes 2490368
  315.9 17.2 %slice-start.21 = ((s8[9633792]{0:T(1024)(128)(4,1)}), s8[4194304]{0:T(1024)(128)(4,1)S(1)}, s32[]{:S(2)}) async-start(s8[9633792]{0:T(1024)(128)(4,1)} %bitcast.113), calls=%async_computation.25 | async-start | bytes 8388608
  315.9 17.2 %slice-start.22 = ((s8[9633792]{0:T(1024)(128)(4,1)}), s8[4194304]{0:T(1024)(128)(4,1)S(1)}, s32[]{:S(2)}) async-start(s8[9633792]{0:T(1024)(128)(4,1)} %bitcast.113), calls=%async_computation.26 | async-start | bytes 8388608
  325.9 7.2 %slice-start.23 = ((s8[9633792]{0:T(1024)(128)(4,1)}), s8[1245184]{0:T(1024)(128)(4,1)S(1)}, s32[]{:S(2)}) async-start(s8[9633792]{0:T(1024)(128)(4,1)} %bitcast.113), calls=%async_computation.27 | async-start | bytes 2490368
  351.2 19.7 %slice-start.12 = ((s8[9633792]{0:T(1024)(128)(4,1)}), s8[4194304]{0:T(1024)(128)(4,1)S(1)}, s32[]{:S(2)}) async-start(s8[9633792]{0:T(1024)(128)(4,1)} %bitcast.107), calls=%async_computation.16 | async-start | bytes 8388608
  351.2 19.7 %slice-start.13 = ((s8[9633792]{0:T(1024)(128)(4,1)}), s8[4194304]{0:T(1024)(128)(4,1)S(1)}, s32[]{:S(2)}) async-start(s8[9633792]{0:T(1024)(128)(4,1)} %bitcast.107), calls=%async_computation.17 | async-start | bytes 8388608
  360.6 10.2 %slice-start.14 = ((s8[9633792]{0:T(1024)(128)(4,1)}), s8[1245184]{0:T(1024)(128)(4,1)S(1)}, s32[]{:S(2)}) async-start(s8[9633792]{0:T(1024)(128)(4,1)} %bitcast.107), calls=%async_computation.18 | async-start | bytes 2490368
  360.6 17.4 %slice-start.6 = ((s8[9633792]{0:T(1024)(128)(4,1)}), s8[4194304]{0:T(1024)(128)(4,1)S(1)}, s32[]{:S(2)}) async-start(s8[9633792]{0:T(1024)(128)(4,1)} %bitcast.103), calls=%async_computation.10 | async-start | bytes 8388608
  360.6 17.4 %slice-start.7 = ((s8[9633792]{0:T(1024)(128)(4,1)}), s8[4194304]{0:T(1024)(128)(4,1)S(1)}, s32[]{:S(2)}) async-start(s8[9633792]{0:T(1024)(128)(4,1)} %bitcast.103), calls=%async_computation.11 | async-start | bytes 8388608
  370.9 7.2 %slice-start.8 = ((s8[9633792]{0:T(1024)(128)(4,1)}), s8[1245184]{0:T(1024)(128)(4,1)S(1)}, s32[]{:S(2)}) async-start(s8[9633792]{0:T(1024)(128)(4,1)} %bitcast.103), calls=%async_computation.12 | async-start | bytes 2490368
  370.9 14.3 %slice-start = ((s8[9633792]{0:T(1024)(128)(4,1)}), s8[4194304]{0:T(1024)(128)(4,1)S(1)}, s32[]{:S(2)}) async-start(s8[9633792]{0:T(1024)(128)(4,1)} %bitcast.99), calls=%async_computation.4 | async-start | bytes 8388608
  370.9 14.3 %slice-start.1 = ((s8[9633792]{0:T(1024)(128)(4,1)}), s8[4194304]{0:T(1024)(128)(4,1)S(1)}, s32[]{:S(2)}) async-start(s8[9633792]{0:T(1024)(128)(4,1)} %bitcast.99), calls=%async_computation.5 | async-start | bytes 8388608
  378.0 7.2 %slice-start.2 = ((s8[9633792]{0:T(1024)(128)(4,1)}), s8[1245184]{0:T(1024)(128)(4,1)S(1)}, s32[]{:S(2)}) async-start(s8[9633792]{0:T(1024)(128)(4,1)} %bitcast.99), calls=%async_computation.6 | async-start | bytes 2490368
  397.7 45.3 %slice-start.24 = ((s8[9633792]{0:T(1024)(128)(4,1)}), s8[1245184]{0:T(1024)(128)(4,1)S(1)}, s32[]{:S(2)}) async-start(s8[9633792]{0:T(1024)(128)(4,1)} %bitcast.115), calls=%async_computation.28 | async-start | bytes 2490368
  402.3 40.7 %slice-start.25 = ((s8[9633792]{0:T(1024)(128)(4,1)}), s8[4194304]{0:T(1024)(128)(4,1)S(1)}, s32[]{:S(2)}) async-start(s8[9633792]{0:T(1024)(128)(4,1)} %bitcast.115), calls=%async_computation.29 | async-start | bytes 8388608
  415.4 27.6 %slice-start.26 = ((s8[9633792]{0:T(1024)(128)(4,1)}), s8[4194304]{0:T(1024)(128)(4,1)S(1)}, s32[]{:S(2)}) async-start(s8[9633792]{0:T(1024)(128)(4,1)} %bitcast.115), calls=%async_computation.30 | async-start | bytes 8388608
  415.4 51.5 %slice-start.18 = ((s8[9633792]{0:T(1024)(128)(4,1)}), s8[4194304]{0:T(1024)(128)(4,1)S(1)}, s32[]{:S(2)}) async-start(s8[9633792]{0:T(1024)(128)(4,1)} %bitcast.111), calls=%async_computation.22 | async-start | bytes 8388608
  429.5 37.4 %slice-start.19 = ((s8[9633792]{0:T(1024)(128)(4,1)}), s8[4194304]{0:T(1024)(128)(4,1)S(1)}, s32[]{:S(2)}) async-start(s8[9633792]{0:T(1024)(128)(4,1)} %bitcast.111), calls=%async_computation.23 | async-start | bytes 8388608
  443.0 23.9 %slice-start.20 = ((s8[9633792]{0:T(1024)(128)(4,1)}), s8[1245184]{0:T(1024)(128)(4,1)S(1)}, s32[]{:S(2)}) async-start(s8[9633792]{0:T(1024)(128)(4,1)} %bitcast.111), calls=%async_computation.24 | async-start | bytes 2490368
  443.1 34.5 %slice-start.15 = ((s8[9633792]{0:T(1024)(128)(4,1)}), s8[4194304]{0:T(1024)(128)(4,1)S(1)}, s32[]{:S(2)}) async-start(s8[9633792]{0:T(1024)(128)(4,1)} %bitcast.109), calls=%async_computation.19 | async-start | bytes 8388608
  443.1 45.2 %slice-start.9 = ((s8[9633792]{0:T(1024)(128)(4,1)}), s8[4194304]{0:T(1024)(128)(4,1)S(1)}, s32[]{:S(2)}) async-start(s8[9633792]{0:T(1024)(128)(4,1)} %bitcast.105), calls=%async_computation.13 | async-start | bytes 8388608
  453.6 24.0 %slice-start.16 = ((s8[9633792]{0:T(1024)(128)(4,1)}), s8[4194304]{0:T(1024)(128)(4,1)S(1)}, s32[]{:S(2)}) async-start(s8[9633792]{0:T(1024)(128)(4,1)} %bitcast.109), calls=%async_computation.20 | async-start | bytes 8388608
  453.6 34.7 %slice-start.10 = ((s8[9633792]{0:T(1024)(128)(4,1)}), s8[4194304]{0:T(1024)(128)(4,1)S(1)}, s32[]{:S(2)}) async-start(s8[9633792]{0:T(1024)(128)(4,1)} %bitcast.105), calls=%async_computation.14 | async-start | bytes 8388608
  466.9 10.6 %slice-start.17 = ((s8[9633792]{0:T(1024)(128)(4,1)}), s8[1245184]{0:T(1024)(128)(4,1)S(1)}, s32[]{:S(2)}) async-start(s8[9633792]{0:T(1024)(128)(4,1)} %bitcast.109), calls=%async_computation.21 | async-start | bytes 2490368
  467.0 21.4 %slice-start.11 = ((s8[9633792]{0:T(1024)(128)(4,1)}), s8[1245184]{0:T(1024)(128)(4,1)S(1)}, s32[]{:S(2)}) async-start(s8[9633792]{0:T(1024)(128)(4,1)} %bitcast.105), calls=%async_computation.15 | async-start | bytes 2490368
  477.6 21.2 %slice-start.3 = ((s8[9633792]{0:T(1024)(128)(4,1)}), s8[4194304]{0:T(1024)(128)(4,1)S(1)}, s32[]{:S(2)}) async-start(s8[9633792]{0:T(1024)(128)(4,1)} %bitcast.101), calls=%async_computation.7 | async-start | bytes 8388608
  477.6 21.2 %slice-start.4 = ((s8[9633792]{0:T(1024)(128)(4,1)}), s8[4194304]{0:T(1024)(128)(4,1)S(1)}, s32[]{:S(2)}) async-start(s8[9633792]{0:T(1024)(128)(4,1)} %bitcast.101), calls=%async_computation.8 | async-start | bytes 8388608
  488.4 10.5 %slice-start.5 = ((s8[9633792]{0:T(1024)(128)(4,1)}), s8[1245184]{0:T(1024)(128)(4,1)S(1)}, s32[]{:S(2)}) async-start(s8[9633792]{0:T(1024)(128)(4,1)} %bitcast.101), calls=%async_computation.9 | async-start | bytes 2490368
  515.4 15.4 %all-to-all-start = ((f32[16,1,9408]{2,1,0:T(1,128)}), f32[16,1,9408]{2,1,0:T(1,128)S(1)}, u32[]{:S(2)}, u32[]{:S(2)}) async-start(f32[16,1,9408]{2,1,0:T(1,128)} %reshape.53), calls=%async_computation | async-start | bytes 1212416 | tf_op jit(solution)/shard_map/all_to_all | solution.py:56
Sparse Core Ops, SparseCore 0:
  9.7 66.7 all-gather.2
  402.4 210.0 all-gather.4
